TPU v7x, 32 devices: a whole 2x2x4 slice. The times are simulated.
32 devices in a mesh: clip: 4 (over z), band: 4 (over x, core), chan: 2 (over y).
Axes of the slice: x: 2, y: 2, z: 4, core: 2. Of those that a mesh axis runs over, the one named last changes fastest.
Arguments:
- frames: bfloat16 [512, 4, 5120], P(None, 'clip', ('band', 'chan')), may hold values from -6 to 6
- weight: bfloat16 [512, 3, 3, 512], P('chan'), may hold values from -0.09375 to 0.09375
- bias: float32 [512], replicated, may hold values from -3 to 3
- cotangent: bfloat16 [512, 4, 5120], P(None, 'clip', ('band', 'chan')), may hold values from -6 to 6
Outputs:
- outputs: bfloat16 [512, 4, 5120], P(None, 'clip', ('band', 'chan'))
- grad_frames: bfloat16 [512, 4, 5120], P(None, 'clip', ('band', 'chan'))
- grad_weight: float32 [512, 3, 3, 512], P('chan')
- grad_bias: float32 [512], P('chan')
All inputs are finite; a program needn't handle non-finite values.
Results may differ from a plain program's by a relative error of at most 0.001.
Values may be sent and summed in bfloat16 or wider, within the bound.
A program may use at most 128 MiB of HBM per device.

v0:
```python
import functools
import math

import jax
import jax.numpy as jnp
from jax import lax
from jax.experimental import pallas as pl
from jax.experimental.pallas import tpu as pltpu
from jax.sharding import PartitionSpec as P

W = 160
MESH = pl.DeviceIdType.MESH
F32 = jnp.float32
BF16 = jnp.bfloat16


def ds(start, size):
    return pl.ds(pl.multiple_of(start, size), size)


def remote(src, dst, send, recv, device):
    return pltpu.make_async_remote_copy(
        src_ref=src, dst_ref=dst, send_sem=send, recv_sem=recv, device_id=device, device_id_type=MESH
    )


def sides(rows):
    wide = rows.astype(F32)
    at = lax.broadcasted_iota(jnp.int32, wide.shape, 0)
    left = jnp.where(at == 0, 0.0, pltpu.roll(wide, 1, 0)).astype(BF16)
    right = jnp.where(at == W - 1, 0.0, pltpu.roll(wide, W - 1, 0)).astype(BF16)
    return left, rows, right


def kernel(
    dims, x_in, g_in, w_ref, bias_in, o_ref, db_ref, out_ref, back_ref,
    xs, gs, dx, xe, ge, kern, acc, share, got1, got2, dbs, dgot, hx, hg, xt_ref, gt_ref, x_ref, g_ref, bias_ref, sems, regs,
):
    clips, bands, chans, rows_o, rows_i, cells, channels, scale = dims
    group = bands * chans
    half = rows_o // 2
    lanes = channels // clips
    width = bands // 2
    units = cells // W
    total = cells * group
    z, b, n = lax.axis_index("clip"), lax.axis_index("band"), lax.axis_index("chan")
    me = b * chans + n
    core = b % 2
    sib = b + 1 - 2 * core
    sib_id = {"band": sib}
    nxt, prv = (me + 1) % group, (me + group - 1) % group
    nxt_id = {"band": nxt // chans, "chan": nxt % chans}
    prv_id = {"band": prv // chans, "chan": prv % chans}
    z0 = z % 2
    inner = (z + 1) // 2 == 1
    near, middle = {"clip": z + 1 - 2 * z0}, {"clip": clips - 1 - z}

    loads = [
        pltpu.make_async_copy(src, dst, regs.at[3 + i])
        for i, (src, dst) in enumerate(((x_in, x_ref), (g_in, g_ref), (bias_in, bias_ref)))
    ]
    for load in loads:
        load.start()
    barrier = pltpu.get_barrier_semaphore()
    targets = [{"clip": (z + k) % clips} for k in range(1, clips)]
    for k in range(1, group):
        to = (me + k) % group
        targets.append({"band": to // chans, "chan": to % chans})
    for target in targets:
        pl.semaphore_signal(barrier, inc=1, device_id=target, device_id_type=MESH)

    def turn(src, dst):
        @pl.loop(0, cells // 128)
        def _(t):
            dst[ds(t * 128, 128), :] = src[:, ds(t * 128, 128)].astype(F32).T.astype(BF16)

    loads[0].wait()
    turn(x_ref, xt_ref)
    loads[1].wait()
    loads[2].wait()
    pl.semaphore_wait(barrier, len(targets))

    started = []
    names = {}

    def pair(key):
        if key not in names:
            names[key] = len(names)
        return sems.at[0, names[key]], sems.at[1, names[key]]

    def send(src, dst, key, device):
        s, r = pair(key)
        copy = remote(src, dst, s, r, device)
        copy.start()
        started.append(copy)

    def arrive(dst, key):
        s, r = pair(key)
        remote(dst, dst, s, r, sib_id).wait_recv()

    def slab(src_n, part, zz):
        return kern.at[:, ds((2 * src_n + part) * half, half), ds(zz * lanes, lanes)]

    keep_w = pltpu.make_async_copy(w_ref, kern.at[:, ds(n * rows_o, rows_o), :], regs.at[0])
    keep_x = pltpu.make_async_copy(xt_ref.at[:, ds(b * rows_i, rows_i)], xs.at[ds(me * cells, cells), :], regs.at[1])
    keep_g = pltpu.make_async_copy(g_ref.at[ds(n * rows_o, rows_o), :], gs.at[:, ds(me * cells, cells)], regs.at[2])

    def x_place(src_b, src_n):
        return xs.at[ds((src_b * chans + src_n) * cells, cells), :]

    def g_place(src_b, src_n):
        return gs.at[:, ds((src_b * chans + src_n) * cells, cells)]

    for m in range(1, chans):
        send(w_ref.at[:, ds(core * half, half), ds(z * lanes, lanes)], slab(n, core, z), ("w", m), {"chan": (n + m) % chans})
    for d in range(1, bands):
        to_b = (b + d) % bands
        send(xt_ref.at[:, ds(to_b * rows_i, rows_i)], x_place(b, n), ("x", d, 0), {"band": to_b})
    for m in range(1, chans):
        to_n = (n + m) % chans
        send(g_ref.at[ds(to_n * rows_o, rows_o), :], g_place(b, n), ("g", 0, m), {"chan": to_n})
        send(xt_ref.at[:, ds(b * rows_i, rows_i)], x_place(b, n), ("x", 0, m), {"chan": to_n})
    own_g = g_ref.at[ds(n * rows_o, rows_o), :]
    for j in range(1, width):
        send(own_g, g_place(b, n), ("g", j, 0), {"band": (b + 2 * j) % bands})
    send(own_g, g_place(b, n), ("f", 0, 0), sib_id)
    keep_x.start()
    keep_g.start()
    keep_w.start()

    def widen(dst, to, rows, size):
        for t, part in enumerate(sides(rows)):
            dst[ds(to, W), t * size:(t + 1) * size] = part

    def widen_block(src):
        @pl.loop(0, units)
        def _(u):
            at = src * cells + u * W
            widen(dx, at + W, xs[ds(at, W), :], rows_i)

    for m in range(1, chans):
        src = (n + chans - m) % chans
        arrive(slab(src, core, z), ("w", m))
        for q in range(1, clips):
            send(slab(src, core, z), slab(src, core, z), ("wz", m, q), {"clip": (z + q) % clips})
        send(slab(src, core, z), slab(src, core, z), ("ws", m, 0), sib_id)
    for d in range(1, bands):
        place = x_place((b + bands - d) % bands, n)
        arrive(place, ("x", d, 0))
        for m in range(1, chans):
            send(place, place, ("x", d, m), {"chan": (n + m) % chans})
    for m in range(1, chans):
        place = g_place(b, (n + chans - m) % chans)
        arrive(place, ("g", 0, m))
        for j in range(1, width):
            send(place, place, ("g", j, m), {"band": (b + 2 * j) % bands})
        send(place, place, ("f", 0, m), sib_id)
    for j in range(1, width):
        place = g_place((b + bands - 2 * j) % bands, n)
        arrive(place, ("g", j, 0))
        send(place, place, ("f", j, 0), sib_id)

    turn(g_ref, gt_ref)
    dx[pl.ds(0, W), :] = jnp.zeros((W, 3 * rows_i), BF16)
    dx[pl.ds(total + W, W), :] = jnp.zeros((W, 3 * rows_i), BF16)

    @pl.loop(0, units)
    def _(u):
        widen(xe, (u + 1) * W, xt_ref[ds(u * W, W), :], channels)
        widen(ge, (u + 1) * W, gt_ref[ds(u * W, W), :], channels)

    keep_x.wait()
    widen_block(me)
    for d in range(1, bands):
        widen_block(((b + bands - d) % bands) * chans + n)
    for m in range(1, chans):
        src_n = (n + chans - m) % chans
        arrive(x_place(b, src_n), ("x", 0, m))
        widen_block(b * chans + src_n)
    for j in range(1, width):
        for m in range(1, chans):
            place = g_place((b + bands - 2 * j) % bands, (n + chans - m) % chans)
            arrive(place, ("g", j, m))
            send(place, place, ("f", j, m), sib_id)
    for d in range(1, bands):
        for m in range(1, chans):
            src_b, src_n = (b + bands - d) % bands, (n + chans - m) % chans
            arrive(x_place(src_b, src_n), ("x", d, m))
            widen_block(src_b * chans + src_n)
    send(xt_ref.at[pl.ds(cells - W, W), :], hx.at[0], ("hx", 0), nxt_id)
    send(gt_ref.at[pl.ds(cells - W, W), :], hg.at[0], ("hg", 0), nxt_id)
    send(xt_ref.at[pl.ds(0, W), :], hx.at[1], ("hx", 1), prv_id)
    send(gt_ref.at[pl.ds(0, W), :], hg.at[1], ("hg", 1), prv_id)
    for j in range(width):
        for m in range(chans):
            arrive(g_place((sib + bands - 2 * j) % bands, (n + chans - m) % chans), ("f", j, m))
    keep_g.wait()

    block = 2 * cells

    def tap_row(a):
        acc2 = acc.at[pl.ds(0, rows_o), pl.ds(0, 3 * rows_i)]
        acc2[...] = jnp.zeros((rows_o, 3 * rows_i), F32)

        @pl.loop(0, group // 2)
        def _(k):
            rows = pl.ds(pl.multiple_of(k * block + a * W, 32), block)
            acc2[...] += jnp.dot(gs[:, ds(k * block, block)], dx[rows, :], preferred_element_type=F32)

        for t in range(3):
            share[3 * a + t] = acc2[:, t * rows_i:(t + 1) * rows_i] * scale

    side = z // 2

    def spot(t, part, bb):
        return o_ref.at[t, ds(part * half, half), ds(bb * rows_i, rows_i)]

    def spread(t, part, step):
        place = spot(t, part, b)
        for j in range(1, width):
            send(place, place, ("xo", t, step, j), {"band": (b + 2 * j) % bands})
        send(place, place, ("c", t, step, 0), sib_id)

    def give(t):
        send(share.at[t], got1.at[t], ("r1", t), near)

    def take(t):
        arrive(got1.at[t], ("r1", t))
        share[t] += got1[t]
        send(share.at[t, ds((1 - side) * half, half), :], got2.at[t], ("r2", t), middle)

    def settle(t):
        arrive(got2.at[t], ("r2", t))
        o_ref[t, ds(side * half, half), ds(b * rows_i, rows_i)] = share[t, ds(side * half, half), :] + got2[t]
        place = spot(t, side, b)
        send(place, place, ("a1", t), middle)
        send(place, place, ("a2", t, 0), near)
        spread(t, side, 0)

    def share_back(t):
        place = spot(t, 1 - side, b)
        arrive(place, ("a1", t))
        send(place, place, ("a2", t, 1), near)
        spread(t, 1 - side, 1)

    def receive(t):
        for step, part in enumerate((side, 1 - side)):
            arrive(spot(t, part, b), ("a2", t, step))
            spread(t, part, step)

    def cross(t):
        for step, part in enumerate((side, 1 - side)):
            for j in range(1, width):
                place = spot(t, part, (b + bands - 2 * j) % bands)
                arrive(place, ("xo", t, step, j))
                send(place, place, ("c", t, step, j), sib_id)

    def finish(t):
        for step, part in enumerate((side, 1 - side)):
            for j in range(width):
                arrive(spot(t, part, (sib + bands - 2 * j) % bands), ("c", t, step, j))

    def conv(a):
        @pl.loop(0, channels // 256)
        def _(t):
            rows = ds(t * 256, 256)
            if a == 0:
                column = jnp.broadcast_to(bias_ref[:, rows], (8, 256)).T[:, :1]
                part = jnp.zeros((256, cells), F32) + column
            else:
                part = acc[rows, :]
            for s in range(3):
                part += lax.dot_general(
                    kern[3 * a + s, rows, :], xe[a * W:a * W + cells, s * channels:(s + 1) * channels],
                    (((1,), (1,)), ((), ())), preferred_element_type=F32,
                )
            if a == 2:
                out_ref[rows, :] = part.astype(BF16)
            else:
                acc[rows, :] = part

    half_cells = cells // 2

    def back(a):
        @pl.loop(0, 2)
        def _(t):
            rows = ds(t * half_cells, half_cells)
            c = 2 - a
            part = jnp.zeros((half_cells, channels), F32)
            if a:
                part = acc[ds(t * half_cells, half_cells), pl.ds(0, channels)]
            for s in range(3):
                part += jnp.dot(
                    ge[pl.ds(pl.multiple_of(c * W + t * half_cells, 32), half_cells), (2 - s) * channels:(3 - s) * channels],
                    kern[3 * a + s], preferred_element_type=F32,
                )
            acc[rows, pl.ds(0, channels)] = part

        if a == 2:
            @pl.loop(0, cells // 128)
            def _(t):
                back_ref[:, ds(t * 128, 128)] = acc[ds(t * 128, 128), pl.ds(0, channels)].T.astype(BF16)

    def bias_sum():
        ones = jnp.ones((8, block), BF16)
        dbs[...] = jnp.zeros((8, rows_o), F32)

        @pl.loop(0, group // 2)
        def _(k):
            dbs[...] += lax.dot_general(
                ones, gs[:, ds(k * block, block)], (((1,), (1,)), ((), ())), preferred_element_type=F32
            )

        for q in range(1, clips):
            send(dbs, dgot.at[q], ("d", q), {"clip": (z + q) % clips})

    def halos():
        for h in range(2):
            arrive(hx.at[h], ("hx", h))
            arrive(hg.at[h], ("hg", h))
            edge = me == (0 if h == 0 else group - 1)
            for src, dst in ((hx, xe), (hg, ge)):
                rows = src[h]
                rows = jnp.where(edge, jnp.zeros_like(rows), rows)
                for t, part in enumerate(sides(rows)):
                    dst[pl.ds(h * (cells + W), W), t * channels:(t + 1) * channels] = part

    def weights():
        for m in range(1, chans):
            src = (n + chans - m) % chans
            for q in range(1, clips):
                zz = (z + clips - q) % clips
                arrive(slab(src, core, zz), ("wz", m, q))
                send(slab(src, core, zz), slab(src, core, zz), ("ws", m, q), sib_id)
        for m in range(1, chans):
            src = (n + chans - m) % chans
            for q in range(clips):
                arrive(slab(src, 1 - core, (z + clips - q) % clips), ("ws", m, q))
        keep_w.wait()

    def matmuls():
        yield halos()
        yield weights()
        for a in range(3):
            yield conv(a)
        for a in range(3):
            yield back(a)

    gathered = list(started)

    def second_half(role):
        started.clear()
        work = matmuls()
        for a in range(3):
            tap_row(a)
            if not role:
                for t in range(3 * a, 3 * a + 3):
                    give(t)
        bias_sum()
        if role:
            for t in range(13):
                for step, lag in ((take, 0), (settle, 1), (share_back, 2), (cross, 4)):
                    if 0 <= t - lag < 9:
                        step(t - lag)
                if t >= 3:
                    next(work, None)
        else:
            for t in range(11):
                for step, lag in ((receive, 0), (cross, 2)):
                    if 0 <= t - lag < 9:
                        step(t - lag)
                if t >= 2:
                    next(work, None)
        for _ in work:
            pass
        for q in range(1, clips):
            arrive(dgot.at[q], ("d", q))
        sums = dbs[...]
        for q in range(1, clips):
            sums = sums + dgot[q]
        db_ref[...] = sums[:1] * scale
        for t in range(9):
            finish(t)
        for copy in started:
            copy.wait_send()

    @pl.when(inner)
    def _():
        second_half(True)

    @pl.when(jnp.logical_not(inner))
    def _():
        second_half(False)

    for copy in gathered:
        copy.wait_send()


def emit(*refs):
    sources, places, sems = refs[:4], refs[4:8], refs[8]
    copies = [pltpu.make_async_copy(src, dst, sems.at[i]) for i, (src, dst) in enumerate(zip(sources, places))]
    for copy in copies:
        copy.start()
    for copy in copies:
        copy.wait()


VM = pl.BlockSpec(memory_space=pltpu.VMEM)


def local(frames, weight, bias, cotangent):
    channels, frame_count, cells = frames.shape
    clips, bands, chans = (lax.axis_size(a) for a in ("clip", "band", "chan"))
    group = bands * chans
    assert frame_count == 1 and cells % W == 0 and clips == 4
    total = cells * group
    scale = 1.0 / math.sqrt(frame_count * clips * total)
    rows_i, rows_o = channels // bands, channels // chans
    x = frames.reshape(channels, cells)
    g = cotangent.reshape(channels, cells)
    wt = jnp.transpose(weight, (1, 2, 0, 3)).reshape(9, rows_o, channels)
    half = rows_o // 2
    width = bands // 2
    copies = (chans - 1) * (1 + clips - 1 + clips) + 2 * width * chans + group + bands * chans + 4 + clips + 9 * (5 + 4 * width) + 8
    limit = (24 << 20) + (total + 2 * W) * 4 * rows_i * 2 + rows_o * total * 2 + rows_o * channels * 72
    shape = jax.ShapeDtypeStruct
    grad, db, outputs, back = pl.pallas_call(
        functools.partial(kernel, (clips, bands, chans, rows_o, rows_i, cells, channels, scale)),
        out_shape=(
            shape((9, rows_o, channels), F32),
            shape((1, rows_o), F32),
            shape((channels, cells), BF16),
            shape((channels, cells), BF16),
        ),
        in_specs=[pl.BlockSpec(memory_space=pltpu.HBM)] * 4,
        out_specs=(VM,) * 4,
        scratch_shapes=[
            pltpu.VMEM((total, rows_i), BF16),
            pltpu.VMEM((rows_o, total), BF16),
            pltpu.VMEM((total + 2 * W, 3 * rows_i), BF16),
            pltpu.VMEM((cells + 2 * W, 3 * channels), BF16),
            pltpu.VMEM((cells + 2 * W, 3 * channels), BF16),
            pltpu.VMEM((9, channels, channels), BF16),
            pltpu.VMEM((max(channels, cells), max(channels, cells)), F32),
            pltpu.VMEM((9, rows_o, rows_i), F32),
            pltpu.VMEM((9, rows_o, rows_i), F32),
            pltpu.VMEM((9, half, rows_i), F32),
            pltpu.VMEM((8, rows_o), F32),
            pltpu.VMEM((clips, 8, rows_o), F32),
            pltpu.VMEM((2, W, channels), BF16),
            pltpu.VMEM((2, W, channels), BF16),
            pltpu.VMEM((cells, channels), BF16),
            pltpu.VMEM((cells, channels), BF16),
            pltpu.VMEM((channels, cells), BF16),
            pltpu.VMEM((channels, cells), BF16),
            pltpu.VMEM((1, channels), F32),
            pltpu.SemaphoreType.DMA((2, copies)),
            pltpu.SemaphoreType.DMA((6,)),
        ],
        compiler_params=pltpu.CompilerParams(collective_id=0, has_side_effects=True, vmem_limit_bytes=min(67000000, limit)),
    )(x, g, wt, bias[None, :])
    results = (grad, db, outputs, back)
    grad, db, outputs, back = pl.pallas_call(
        emit,
        out_shape=tuple(shape(r.shape, r.dtype) for r in results),
        in_specs=[VM] * 4,
        out_specs=(pl.BlockSpec(memory_space=pl.ANY),) * 4,
        scratch_shapes=[pltpu.SemaphoreType.DMA((4,))],
        compiler_params=pltpu.CompilerParams(vmem_limit_bytes=16 << 20),
    )(*results)
    outputs = outputs.reshape(frames.shape)
    grad_frames = back.reshape(frames.shape)
    grad_weight = jnp.transpose(grad.reshape(3, 3, rows_o, channels), (2, 0, 1, 3))
    return outputs, grad_frames, grad_weight, db[0]


def solution(mesh):
    cells = P(None, "clip", ("band", "chan"))
    taps = P("chan", None, None, None)
    return jax.shard_map(
        local, mesh=mesh, in_specs=(cells, taps, P(), cells), out_specs=(cells, cells, taps, P("chan")), check_vma=False
    )
```

profile of v0, /device:TPU:0, one launch (start us, length us, event | category | flops | bytes accessed | tf_op | source)
XLA Modules:
  0.0 93.4 jit_solution(10125400868554486635)
XLA Ops:
  0.6 0.0 copy-start
  0.6 1.7 %copy-done = bf16[256,3,3,512]{3,0,2,1:T(8,128)(2,1)S(1)} copy-done((bf16[256,3,3,512]{3,0,2,1:T(8,128)(2,1)S(1)}, bf16[256,3,3,512]{3,0,2,1:T(8,128)(2,1)}, u32[]{:S(2)}) %copy-start) | copy-done | bytes 2359320
  2.3 0.0 copy-start.1
  2.3 1.1 %copy-done.1 = bf16[512,1,640]{2,0,1:T(8,128)(2,1)S(1)} copy-done((bf16[512,1,640]{2,0,1:T(8,128)(2,1)S(1)}, bf16[512,1,640]{2,0,1:T(8,128)(2,1)}, u32[]{:S(2)}) %copy-start.1) | copy-done | bytes 655384
  3.4 0.0 copy-start.2
  3.4 1.1 %copy-done.2 = bf16[512,1,640]{2,0,1:T(8,128)(2,1)S(1)} copy-done((bf16[512,1,640]{2,0,1:T(8,128)(2,1)S(1)}, bf16[512,1,640]{2,0,1:T(8,128)(2,1)}, u32[]{:S(2)}) %copy-start.2) | copy-done | bytes 655384
  4.5 0.0 copy-start.3
  4.5 0.7 copy-done.3
  5.2 85.6 %shard_map.75 = (f32[9,256,512]{2,1,0:T(8,128)S(1)}, f32[1,256]{1,0:T(1,128)S(1)}, bf16[512,640]{1,0:T(8,128)(2,1)S(1)}, bf16[512,640]{1,0:T(8,128)(2,1)S(1)}) custom-call(bf16[512,640]{1,0:T(8,128)(2,1)S(1)} %bitcast.13, bf16[512,640]{1,0:T(8,128)(2,1)S(1)} %bitcast.14, bf16[9,256,512]{2,1,0:T(8,128)(2,1)S(1)} %bitcast.12, f32[1,512]{1,0:T(1,128)S(1)} %bitcast.15), custom_call_target="tpu_custom_call" | custom-call | tf_op jit(solution)/shard_map/pallas_call | solution.py:427
  90.8 2.6 %shard_map.76 = (f32[9,256,512]{2,1,0:T(8,128)}, f32[1,256]{1,0:T(1,128)}, bf16[512,640]{1,0:T(8,128)(2,1)}, bf16[512,640]{1,0:T(8,128)(2,1)}) custom-call(f32[9,256,512]{2,1,0:T(8,128)S(1)} %get-tuple-element.12.refs_0_, f32[1,256]{1,0:T(1,128)S(1)} %get-tuple-element.13.refs_1_, bf16[512,640]{1,0:T(8,128)(2,1)S(1)} %get-tuple-element.14.refs_2_, ...), custom_call_target="tpu_custom_call" | custom-call | tf_op jit(solution)/shard_map/pallas_call | solution.py:463
Async XLA Ops:
  0.6 1.7 %copy-start = (bf16[256,3,3,512]{3,0,2,1:T(8,128)(2,1)S(1)}, bf16[256,3,3,512]{3,0,2,1:T(8,128)(2,1)}, u32[]{:S(2)}) copy-start(bf16[256,3,3,512]{3,0,2,1:T(8,128)(2,1)} %param.5) | copy-start | bytes 7077892
  2.3 1.1 %copy-start.1 = (bf16[512,1,640]{2,0,1:T(8,128)(2,1)S(1)}, bf16[512,1,640]{2,0,1:T(8,128)(2,1)}, u32[]{:S(2)}) copy-start(bf16[512,1,640]{2,0,1:T(8,128)(2,1)} %param.4) | copy-start | bytes 1966084
  3.4 1.1 %copy-start.2 = (bf16[512,1,640]{2,0,1:T(8,128)(2,1)S(1)}, bf16[512,1,640]{2,0,1:T(8,128)(2,1)}, u32[]{:S(2)}) copy-start(bf16[512,1,640]{2,0,1:T(8,128)(2,1)} %param.7) | copy-start | bytes 1966084
  4.5 0.7 copy-start.3
where the time goes:
time: 93.7 us; the launch traced here: 93.4 us
  Pallas kernels  88.2 us (94%)
  local copies, waits for them, and re-layouts  4.51 us (5%)
    pallas_call x1, Pallas kernels, local(): pl.pallas_call(functools.partial(kernel, (clips, bands, chans, rows_o, ro...  85.6 us
    unnamed x8, local copies, waits for them, and re-layouts  4.51 us
    pallas_call x1, Pallas kernels, local(): pl.pallas_call(emit, out_shape=tuple((shape(r.shape, r.dtype) for r in re...  2.63 us

commit v1 on v0

--- a/solution.py
+++ b/solution.py
@@ -32,9 +32,31 @@
     return left, rows, right
 
 
+def encode(dst, at, value):
+    rows, lanes = value.shape
+    wide = value.reshape(rows // 16, 16, lanes)
+    top = jnp.maximum(jnp.max(jnp.abs(wide), axis=0), 1e-35).astype(BF16)
+    u = wide * (1.0 / top.astype(F32))
+    power = u * u
+    power = power * power
+    power = power * power
+    code = jnp.where(u < 0.0, -power, power).reshape(rows, lanes)
+    dst[(*at, pl.ds(0, 16), slice(None))] = top
+    dst[(*at, pl.ds(16, rows), slice(None))] = code.astype(BF16)
+
+
+def decode(block):
+    rows, lanes = block.shape
+    top = block[:16].astype(F32)
+    code = block[16:].astype(F32)
+    root = jnp.exp(jnp.log(jnp.abs(code)) * 0.125)
+    root = jnp.where(code > 0.0, root, jnp.where(code < 0.0, -root, 0.0))
+    return (root.reshape(rows // 16 - 1, 16, lanes) * top).reshape(rows - 16, lanes)
+
+
 def kernel(
     dims, x_in, g_in, w_ref, bias_in, o_ref, db_ref, out_ref, back_ref,
-    xs, gs, dx, xe, ge, kern, acc, share, got1, got2, dbs, dgot, hx, hg, xt_ref, gt_ref, x_ref, g_ref, bias_ref, sems, regs,
+    xs, gs, dx, xe, ge, kern, acc, share, coded, got1, got2, dbs, dgot, hx, hg, xt_ref, gt_ref, x_ref, g_ref, bias_ref, sems, regs,
 ):
     clips, bands, chans, rows_o, rows_i, cells, channels, scale = dims
     group = bands * chans
@@ -213,7 +235,7 @@
     side = z // 2
 
     def spot(t, part, bb):
-        return o_ref.at[t, ds(part * half, half), ds(bb * rows_i, rows_i)]
+        return o_ref.at[t, part, :, ds(bb * rows_i, rows_i)]
 
     def spread(t, part, step):
         place = spot(t, part, b)
@@ -222,19 +244,24 @@
         send(place, place, ("c", t, step, 0), sib_id)
 
     def give(t):
-        send(share.at[t], got1.at[t], ("r1", t), near)
+        for part in range(2):
+            encode(coded, (t, part), share[t, part * half:(part + 1) * half, :])
+        send(coded.at[t], got1.at[t], ("r1", t), near)
 
     def take(t):
         arrive(got1.at[t], ("r1", t))
-        share[t] += got1[t]
-        send(share.at[t, ds((1 - side) * half, half), :], got2.at[t], ("r2", t), middle)
+        for part in range(2):
+            share[t, part * half:(part + 1) * half, :] += decode(got1[t, part])
+        encode(coded, (t, 0), share[t, ds((1 - side) * half, half), :])
+        send(coded.at[t, 0], got2.at[t], ("r2", t), middle)
 
     def settle(t):
         arrive(got2.at[t], ("r2", t))
-        o_ref[t, ds(side * half, half), ds(b * rows_i, rows_i)] = share[t, ds(side * half, half), :] + got2[t]
+        encode(coded, (t, 1), share[t, ds(side * half, half), :] + decode(got2[t]))
         place = spot(t, side, b)
-        send(place, place, ("a1", t), middle)
-        send(place, place, ("a2", t, 0), near)
+        place[...] = coded[t, 1]
+        send(coded.at[t, 1], place, ("a1", t), middle)
+        send(coded.at[t, 1], place, ("a2", t, 0), near)
         spread(t, side, 0)
 
     def share_back(t):
@@ -397,10 +424,26 @@
 
 
 def emit(*refs):
-    sources, places, sems = refs[:4], refs[4:8], refs[8]
-    copies = [pltpu.make_async_copy(src, dst, sems.at[i]) for i, (src, dst) in enumerate(zip(sources, places))]
+    sources, places, wide, sems = refs[:4], refs[4:8], refs[8], refs[9]
+    copies = [pltpu.make_async_copy(src, dst, sems.at[i]) for i, (src, dst) in enumerate(zip(sources[1:], places[1:]))]
     for copy in copies:
         copy.start()
+    taps, parts, rows, _ = sources[0].shape
+    rows -= 16
+
+    def out(t):
+        return pltpu.make_async_copy(wide.at[t], places[0].at[t], sems.at[3 + t])
+
+    @pl.loop(0, taps)
+    def _(t):
+        for part in range(parts):
+            wide[t, part * rows:(part + 1) * rows, :] = decode(sources[0][t, part])
+        out(t).start()
+
+    @pl.loop(0, taps)
+    def _(t):
+        out(t).wait()
+
     for copy in copies:
         copy.wait()
 
@@ -424,13 +467,14 @@
     copies = (chans - 1) * (1 + clips - 1 + clips) + 2 * width * chans + group + bands * chans + 4 + clips + 9 * (5 + 4 * width) + 8
     limit = (24 << 20) + (total + 2 * W) * 4 * rows_i * 2 + rows_o * total * 2 + rows_o * channels * 72
     shape = jax.ShapeDtypeStruct
+    result = pltpu.VMEM if limit < (50 << 20) else shape
     grad, db, outputs, back = pl.pallas_call(
         functools.partial(kernel, (clips, bands, chans, rows_o, rows_i, cells, channels, scale)),
         out_shape=(
-            shape((9, rows_o, channels), F32),
-            shape((1, rows_o), F32),
-            shape((channels, cells), BF16),
-            shape((channels, cells), BF16),
+            result((9, 2, half + 16, channels), BF16),
+            result((1, rows_o), F32),
+            result((channels, cells), BF16),
+            result((channels, cells), BF16),
         ),
         in_specs=[pl.BlockSpec(memory_space=pltpu.HBM)] * 4,
         out_specs=(VM,) * 4,
@@ -443,8 +487,9 @@
             pltpu.VMEM((9, channels, channels), BF16),
             pltpu.VMEM((max(channels, cells), max(channels, cells)), F32),
             pltpu.VMEM((9, rows_o, rows_i), F32),
-            pltpu.VMEM((9, rows_o, rows_i), F32),
-            pltpu.VMEM((9, half, rows_i), F32),
+            pltpu.VMEM((9, 2, half + 16, rows_i), BF16),
+            pltpu.VMEM((9, 2, half + 16, rows_i), BF16),
+            pltpu.VMEM((9, half + 16, rows_i), BF16),
             pltpu.VMEM((8, rows_o), F32),
             pltpu.VMEM((clips, 8, rows_o), F32),
             pltpu.VMEM((2, W, channels), BF16),
@@ -458,14 +503,14 @@
             pltpu.SemaphoreType.DMA((6,)),
         ],
         compiler_params=pltpu.CompilerParams(collective_id=0, has_side_effects=True, vmem_limit_bytes=min(67000000, limit)),
-    )(x, g, wt, bias[None, :])
+    )(*(pltpu.with_memory_space_constraint(v, pltpu.HBM) for v in (x, g, wt, bias[None, :])))
     results = (grad, db, outputs, back)
     grad, db, outputs, back = pl.pallas_call(
         emit,
-        out_shape=tuple(shape(r.shape, r.dtype) for r in results),
+        out_shape=(shape((9, rows_o, channels), F32),) + tuple(shape(r.shape, r.dtype) for r in results[1:]),
         in_specs=[VM] * 4,
         out_specs=(pl.BlockSpec(memory_space=pl.ANY),) * 4,
-        scratch_shapes=[pltpu.SemaphoreType.DMA((4,))],
+        scratch_shapes=[pltpu.VMEM((9, rows_o, channels), F32), pltpu.SemaphoreType.DMA((12,))],
         compiler_params=pltpu.CompilerParams(vmem_limit_bytes=16 << 20),
     )(*results)
     outputs = outputs.reshape(frames.shape)

time: 93.7 us -> 82 us (0.88)
  Pallas kernels: 88.2 us -> 81.1 us
  local copies, waits for them, and re-layouts: 4.51 us -> 0 us
    pallas_call x1, Pallas kernels: 85.6 us -> 78.1 us  [local(): pl.pallas_call(functools.partial(kernel, (clips, bands, chans, rows_o, ro...]
    unnamed x8 -> x0, local copies, waits for them, and re-layouts: 4.51 us -> none
where the time goes in v1:
time: 82 us; the launch traced here: 81.9 us
  Pallas kernels  81.1 us (99%)
    pallas_call x1, Pallas kernels, local(): pl.pallas_call(functools.partial(kernel, (clips, bands, chans, rows_o, ro...  78.1 us
    pallas_call x1, Pallas kernels, local(): pl.pallas_call(emit, out_shape=(shape((9, rows_o, channels), F32),) + tup...  3.02 us

profile of v1, /device:TPU:0, one launch (start us, length us, event | category | flops | bytes accessed | tf_op | source)
XLA Modules:
  0.0 81.9 jit_solution(12167268583706616307)
XLA Ops:
  0.6 78.1 %shard_map.75 = (bf16[9,2,144,512]{3,2,1,0:T(8,128)(2,1)S(1)}, f32[1,256]{1,0:T(1,128)S(1)}, bf16[512,640]{1,0:T(8,128)(2,1)S(1)}, bf16[512,640]{1,0:T(8,128)(2,1)S(1)}) custom-call(bf16[512,640]{1,0:T(8,128)(2,1)} %bitcast.13, bf16[512,640]{1,0:T(8,128)(2,1)} %bitcast.14, bf16[9,256,512]{2,1,0:T(8,128)(2,1)} %bitcast.12, f32[1,512]{1,0:T(1,128)} %bitcast.15), custom_call_target="tpu_custom_call" | custom-call | tf_op jit(solution)/shard_map/pallas_call | solution.py:471
  78.7 3.0 %shard_map.76 = (f32[9,256,512]{2,1,0:T(8,128)}, f32[1,256]{1,0:T(1,128)}, bf16[512,640]{1,0:T(8,128)(2,1)}, bf16[512,640]{1,0:T(8,128)(2,1)}) custom-call(bf16[9,2,144,512]{3,2,1,0:T(8,128)(2,1)S(1)} %get-tuple-element.12.refs_0_, f32[1,256]{1,0:T(1,128)S(1)} %get-tuple-element.13.refs_1_, bf16[512,640]{1,0:T(8,128)(2,1)S(1)} %get-tuple-element.14.refs_2_, ...), custom_call_target="tpu_custom_call" | custom-call | tf_op jit(solution)/shard_map/pallas_call | solution.py:508

commit v2 on v1

--- a/solution.py
+++ b/solution.py
@@ -56,7 +56,7 @@
 
 def kernel(
     dims, x_in, g_in, w_ref, bias_in, o_ref, db_ref, out_ref, back_ref,
-    xs, gs, dx, xe, ge, kern, acc, share, coded, got1, got2, dbs, dgot, hx, hg, xt_ref, gt_ref, x_ref, g_ref, bias_ref, sems, regs,
+    xs, gs, dx, xe, ge, kern, acc_f, acc_b, share, coded, got1, got2, dbs, dgot, hx, hg, xt_ref, gt_ref, x_ref, g_ref, bias_ref, sems, regs,
 ):
     clips, bands, chans, rows_o, rows_i, cells, channels, scale = dims
     group = bands * chans
@@ -64,6 +64,8 @@
     lanes = channels // clips
     width = bands // 2
     units = cells // W
+    split = chans == 2 and rows_o % 256 == 0
+    cut = -(-W // 128) * 128
     total = cells * group
     z, b, n = lax.axis_index("clip"), lax.axis_index("band"), lax.axis_index("chan")
     me = b * chans + n
@@ -160,17 +162,74 @@
             at = src * cells + u * W
             widen(dx, at + W, xs[ds(at, W), :], rows_i)
 
+    def conv_part(start, count, lo, hi, taps, seed, last):
+        @pl.loop(0, count)
+        def _(t):
+            at, rows = ds(t * 256, 256), ds(start + t * 256, 256)
+            if seed:
+                part = acc_f[at, lo:hi]
+            else:
+                column = jnp.broadcast_to(bias_ref[:, rows], (8, 256)).T[:, :1]
+                part = jnp.zeros((256, hi - lo), F32) + column
+            for a in taps:
+                for s in range(3):
+                    part += lax.dot_general(
+                        kern[3 * a + s, rows, :], xe[a * W + lo:a * W + hi, s * channels:(s + 1) * channels],
+                        (((1,), (1,)), ((), ())), preferred_element_type=F32,
+                    )
+            if last:
+                out_ref[rows, lo:hi] = part.astype(BF16)
+            else:
+                acc_f[at, lo:hi] = part
+
+    def back_part(start, size, lo, hi, rows, seed):
+        part = acc_b[lo:hi, :] if seed else jnp.zeros((hi - lo, channels), F32)
+        for c in rows:
+            for s in range(3):
+                cols = pl.ds(pl.multiple_of((2 - s) * channels + start, 128), size)
+                part += jnp.dot(
+                    ge[c * W + lo:c * W + hi, cols], kern[3 * (2 - c) + s, pl.ds(pl.multiple_of(start, 16), size), :],
+                    preferred_element_type=F32,
+                )
+        acc_b[lo:hi, :] = part
+
+    own, other, stripe = n * rows_o, (1 - n) * rows_o, rows_o // 256
+
+    def conv_early():
+        if split:
+            keep_w.wait()
+            conv_part(own, stripe, 0, cut, (1, 2), False, False)
+            conv_part(own, stripe, cut, cells - cut, (0, 1, 2), False, True)
+            conv_part(own, stripe, cells - cut, cells, (0, 1), False, False)
+
+    def back_early():
+        if split:
+            back_part(own, rows_o, 0, W, (1, 2), False)
+            back_part(own, rows_o, W, cells - W, (0, 1, 2), False)
+            back_part(own, rows_o, cells - W, cells, (0, 1), False)
+
+    turn(g_ref, gt_ref)
+    dx[pl.ds(0, W), :] = jnp.zeros((W, 3 * rows_i), BF16)
+    dx[pl.ds(total + W, W), :] = jnp.zeros((W, 3 * rows_i), BF16)
+
+    @pl.loop(0, units)
+    def _(u):
+        widen(xe, (u + 1) * W, xt_ref[ds(u * W, W), :], channels)
+        widen(ge, (u + 1) * W, gt_ref[ds(u * W, W), :], channels)
+
     for m in range(1, chans):
         src = (n + chans - m) % chans
         arrive(slab(src, core, z), ("w", m))
         for q in range(1, clips):
             send(slab(src, core, z), slab(src, core, z), ("wz", m, q), {"clip": (z + q) % clips})
         send(slab(src, core, z), slab(src, core, z), ("ws", m, 0), sib_id)
+    conv_early()
     for d in range(1, bands):
         place = x_place((b + bands - d) % bands, n)
         arrive(place, ("x", d, 0))
         for m in range(1, chans):
             send(place, place, ("x", d, m), {"chan": (n + m) % chans})
+    back_early()
     for m in range(1, chans):
         place = g_place(b, (n + chans - m) % chans)
         arrive(place, ("g", 0, m))
@@ -181,15 +240,6 @@
         place = g_place((b + bands - 2 * j) % bands, n)
         arrive(place, ("g", j, 0))
         send(place, place, ("f", j, 0), sib_id)
-
-    turn(g_ref, gt_ref)
-    dx[pl.ds(0, W), :] = jnp.zeros((W, 3 * rows_i), BF16)
-    dx[pl.ds(total + W, W), :] = jnp.zeros((W, 3 * rows_i), BF16)
-
-    @pl.loop(0, units)
-    def _(u):
-        widen(xe, (u + 1) * W, xt_ref[ds(u * W, W), :], channels)
-        widen(ge, (u + 1) * W, gt_ref[ds(u * W, W), :], channels)
 
     keep_x.wait()
     widen_block(me)
@@ -221,16 +271,20 @@
     block = 2 * cells
 
     def tap_row(a):
-        acc2 = acc.at[pl.ds(0, rows_o), pl.ds(0, 3 * rows_i)]
-        acc2[...] = jnp.zeros((rows_o, 3 * rows_i), F32)
-
-        @pl.loop(0, group // 2)
-        def _(k):
-            rows = pl.ds(pl.multiple_of(k * block + a * W, 32), block)
-            acc2[...] += jnp.dot(gs[:, ds(k * block, block)], dx[rows, :], preferred_element_type=F32)
-
+        if total <= 8192:
+            rows = jnp.dot(gs[...], dx[a * W:a * W + total, :], preferred_element_type=F32)
+        else:
+            held = acc_b.at[pl.ds(0, rows_o), pl.ds(0, 3 * rows_i)]
+            held[...] = jnp.zeros((rows_o, 3 * rows_i), F32)
+
+            @pl.loop(0, group // 2)
+            def _(k):
+                at = pl.ds(pl.multiple_of(k * block + a * W, 32), block)
+                held[...] += jnp.dot(gs[:, ds(k * block, block)], dx[at, :], preferred_element_type=F32)
+
+            rows = held[...]
         for t in range(3):
-            share[3 * a + t] = acc2[:, t * rows_i:(t + 1) * rows_i] * scale
+            share[3 * a + t] = rows[:, t * rows_i:(t + 1) * rows_i] * scale
 
     side = z // 2
 
@@ -286,47 +340,6 @@
         for step, part in enumerate((side, 1 - side)):
             for j in range(width):
                 arrive(spot(t, part, (sib + bands - 2 * j) % bands), ("c", t, step, j))
-
-    def conv(a):
-        @pl.loop(0, channels // 256)
-        def _(t):
-            rows = ds(t * 256, 256)
-            if a == 0:
-                column = jnp.broadcast_to(bias_ref[:, rows], (8, 256)).T[:, :1]
-                part = jnp.zeros((256, cells), F32) + column
-            else:
-                part = acc[rows, :]
-            for s in range(3):
-                part += lax.dot_general(
-                    kern[3 * a + s, rows, :], xe[a * W:a * W + cells, s * channels:(s + 1) * channels],
-                    (((1,), (1,)), ((), ())), preferred_element_type=F32,
-                )
-            if a == 2:
-                out_ref[rows, :] = part.astype(BF16)
-            else:
-                acc[rows, :] = part
-
-    half_cells = cells // 2
-
-    def back(a):
-        @pl.loop(0, 2)
-        def _(t):
-            rows = ds(t * half_cells, half_cells)
-            c = 2 - a
-            part = jnp.zeros((half_cells, channels), F32)
-            if a:
-                part = acc[ds(t * half_cells, half_cells), pl.ds(0, channels)]
-            for s in range(3):
-                part += jnp.dot(
-                    ge[pl.ds(pl.multiple_of(c * W + t * half_cells, 32), half_cells), (2 - s) * channels:(3 - s) * channels],
-                    kern[3 * a + s], preferred_element_type=F32,
-                )
-            acc[rows, pl.ds(0, channels)] = part
-
-        if a == 2:
-            @pl.loop(0, cells // 128)
-            def _(t):
-                back_ref[:, ds(t * 128, 128)] = acc[ds(t * 128, 128), pl.ds(0, channels)].T.astype(BF16)
 
     def bias_sum():
         ones = jnp.ones((8, block), BF16)
@@ -363,15 +376,29 @@
             src = (n + chans - m) % chans
             for q in range(clips):
                 arrive(slab(src, 1 - core, (z + clips - q) % clips), ("ws", m, q))
-        keep_w.wait()
+        if not split:
+            keep_w.wait()
+
+    def back_out():
+        @pl.loop(0, cells // 128)
+        def _(t):
+            back_ref[:, ds(t * 128, 128)] = acc_b[ds(t * 128, 128), :].T.astype(BF16)
 
     def matmuls():
+        yield bias_sum()
         yield halos()
+        first, size, count = (other, rows_o, stripe) if split else (0, channels, channels // 256)
+        if split:
+            yield conv_part(own, stripe, 0, cut, (0,), True, True)
+            yield conv_part(own, stripe, cells - cut, cells, (2,), True, True)
+            yield back_part(own, rows_o, 0, W, (0,), True)
+            yield back_part(own, rows_o, cells - W, cells, (2,), True)
         yield weights()
-        for a in range(3):
-            yield conv(a)
-        for a in range(3):
-            yield back(a)
+        for lo, hi in ((0, cut), (cut, cells - cut), (cells - cut, cells)):
+            yield conv_part(first, count, lo, hi, (0, 1, 2), False, True)
+        for lo in (0, cells // 2):
+            yield back_part(first, size, lo, lo + cells // 2, (0, 1, 2), split)
+        yield back_out()
 
     gathered = list(started)
 
@@ -383,21 +410,20 @@
             if not role:
                 for t in range(3 * a, 3 * a + 3):
                     give(t)
-        bias_sum()
         if role:
             for t in range(13):
                 for step, lag in ((take, 0), (settle, 1), (share_back, 2), (cross, 4)):
                     if 0 <= t - lag < 9:
                         step(t - lag)
-                if t >= 3:
-                    next(work, None)
+                next(work, None)
         else:
+            for _ in range(3):
+                next(work, None)
             for t in range(11):
                 for step, lag in ((receive, 0), (cross, 2)):
                     if 0 <= t - lag < 9:
                         step(t - lag)
-                if t >= 2:
-                    next(work, None)
+                next(work, None)
         for _ in work:
             pass
         for q in range(1, clips):
@@ -485,7 +511,8 @@
             pltpu.VMEM((cells + 2 * W, 3 * channels), BF16),
             pltpu.VMEM((cells + 2 * W, 3 * channels), BF16),
             pltpu.VMEM((9, channels, channels), BF16),
-            pltpu.VMEM((max(channels, cells), max(channels, cells)), F32),
+            pltpu.VMEM((rows_o, cells), F32),
+            pltpu.VMEM((cells, channels), F32),
             pltpu.VMEM((9, rows_o, rows_i), F32),
             pltpu.VMEM((9, 2, half + 16, rows_i), BF16),
             pltpu.VMEM((9, 2, half + 16, rows_i), BF16),

time: 82 us -> 83.9 us (1.023)
  Pallas kernels: 81.1 us -> 82.9 us
    pallas_call x1, Pallas kernels: 78.1 us -> 79.9 us  [local(): pl.pallas_call(functools.partial(kernel, (clips, bands, chans, rows_o, ro...]
where the time goes in v2:
time: 83.9 us; the launch traced here: 83.7 us
  Pallas kernels  82.9 us (99%)
    pallas_call x1, Pallas kernels, local(): pl.pallas_call(functools.partial(kernel, (clips, bands, chans, rows_o, ro...  79.9 us
    pallas_call x1, Pallas kernels, local(): pl.pallas_call(emit, out_shape=(shape((9, rows_o, channels), F32),) + tup...  3.02 us

profile of v2, /device:TPU:0, one launch (start us, length us, event | category | flops | bytes accessed | tf_op | source)
XLA Modules:
  0.0 83.7 jit_solution(3520488197551625574)
XLA Ops:
  0.6 79.9 %shard_map.75 = (bf16[9,2,144,512]{3,2,1,0:T(8,128)(2,1)S(1)}, f32[1,256]{1,0:T(1,128)S(1)}, bf16[512,640]{1,0:T(8,128)(2,1)S(1)}, bf16[512,640]{1,0:T(8,128)(2,1)S(1)}) custom-call(bf16[512,640]{1,0:T(8,128)(2,1)} %bitcast.13, bf16[512,640]{1,0:T(8,128)(2,1)} %bitcast.14, bf16[9,256,512]{2,1,0:T(8,128)(2,1)} %bitcast.12, f32[1,512]{1,0:T(1,128)} %bitcast.15), custom_call_target="tpu_custom_call" | custom-call | tf_op jit(solution)/shard_map/pallas_call | solution.py:497
  80.5 3.0 %shard_map.76 = (f32[9,256,512]{2,1,0:T(8,128)}, f32[1,256]{1,0:T(1,128)}, bf16[512,640]{1,0:T(8,128)(2,1)}, bf16[512,640]{1,0:T(8,128)(2,1)}) custom-call(bf16[9,2,144,512]{3,2,1,0:T(8,128)(2,1)S(1)} %get-tuple-element.12.refs_0_, f32[1,256]{1,0:T(1,128)S(1)} %get-tuple-element.13.refs_1_, bf16[512,640]{1,0:T(8,128)(2,1)S(1)} %get-tuple-element.14.refs_2_, ...), custom_call_target="tpu_custom_call" | custom-call | tf_op jit(solution)/shard_map/pallas_call | solution.py:535

commit v3 on v2

--- a/solution.py
+++ b/solution.py
@@ -56,7 +56,7 @@
 
 def kernel(
     dims, x_in, g_in, w_ref, bias_in, o_ref, db_ref, out_ref, back_ref,
-    xs, gs, dx, xe, ge, kern, acc_f, acc_b, share, coded, got1, got2, dbs, dgot, hx, hg, xt_ref, gt_ref, x_ref, g_ref, bias_ref, sems, regs,
+    xs, gs, dx, xe, ge, kern, acc_f, acc_o, acc_b, share, coded, final, got1, got2, dbs, dgot, hx, hg, xt_ref, gt_ref, x_ref, g_ref, bias_ref, sems, regs,
 ):
     clips, bands, chans, rows_o, rows_i, cells, channels, scale = dims
     group = bands * chans
@@ -123,7 +123,10 @@
         remote(dst, dst, s, r, sib_id).wait_recv()
 
     def slab(src_n, part, zz):
-        return kern.at[:, ds((2 * src_n + part) * half, half), ds(zz * lanes, lanes)]
+        return kern.at[pl.ds(0, 6), ds((2 * src_n + part) * half, half), ds(zz * lanes, lanes)]
+
+    def late(src_n, part):
+        return kern.at[pl.ds(6, 3), ds((2 * src_n + part) * half, half), :]
 
     keep_w = pltpu.make_async_copy(w_ref, kern.at[:, ds(n * rows_o, rows_o), :], regs.at[0])
     keep_x = pltpu.make_async_copy(xt_ref.at[:, ds(b * rows_i, rows_i)], xs.at[ds(me * cells, cells), :], regs.at[1])
@@ -136,7 +139,7 @@
         return gs.at[:, ds((src_b * chans + src_n) * cells, cells)]
 
     for m in range(1, chans):
-        send(w_ref.at[:, ds(core * half, half), ds(z * lanes, lanes)], slab(n, core, z), ("w", m), {"chan": (n + m) % chans})
+        send(w_ref.at[pl.ds(0, 6), ds(core * half, half), ds(z * lanes, lanes)], slab(n, core, z), ("w", m), {"chan": (n + m) % chans})
     for d in range(1, bands):
         to_b = (b + d) % bands
         send(xt_ref.at[:, ds(to_b * rows_i, rows_i)], x_place(b, n), ("x", d, 0), {"band": to_b})
@@ -162,12 +165,12 @@
             at = src * cells + u * W
             widen(dx, at + W, xs[ds(at, W), :], rows_i)
 
-    def conv_part(start, count, lo, hi, taps, seed, last):
+    def conv_part(acc, start, count, lo, hi, taps, seed, last):
         @pl.loop(0, count)
         def _(t):
             at, rows = ds(t * 256, 256), ds(start + t * 256, 256)
             if seed:
-                part = acc_f[at, lo:hi]
+                part = acc[at, lo:hi]
             else:
                 column = jnp.broadcast_to(bias_ref[:, rows], (8, 256)).T[:, :1]
                 part = jnp.zeros((256, hi - lo), F32) + column
@@ -180,7 +183,7 @@
             if last:
                 out_ref[rows, lo:hi] = part.astype(BF16)
             else:
-                acc_f[at, lo:hi] = part
+                acc[at, lo:hi] = part
 
     def back_part(start, size, lo, hi, rows, seed):
         part = acc_b[lo:hi, :] if seed else jnp.zeros((hi - lo, channels), F32)
@@ -198,9 +201,9 @@
     def conv_early():
         if split:
             keep_w.wait()
-            conv_part(own, stripe, 0, cut, (1, 2), False, False)
-            conv_part(own, stripe, cut, cells - cut, (0, 1, 2), False, True)
-            conv_part(own, stripe, cells - cut, cells, (0, 1), False, False)
+            conv_part(acc_f, own, stripe, 0, cut, (1, 2), False, False)
+            conv_part(acc_f, own, stripe, cut, cells - cut, (0, 1, 2), False, True)
+            conv_part(acc_f, own, stripe, cells - cut, cells, (0, 1), False, False)
 
     def back_early():
         if split:
@@ -263,6 +266,8 @@
     send(gt_ref.at[pl.ds(cells - W, W), :], hg.at[0], ("hg", 0), nxt_id)
     send(xt_ref.at[pl.ds(0, W), :], hx.at[1], ("hx", 1), prv_id)
     send(gt_ref.at[pl.ds(0, W), :], hg.at[1], ("hg", 1), prv_id)
+    for m in range(1, chans):
+        send(w_ref.at[pl.ds(6, 3), ds(core * half, half), :], late(n, core), ("wl", m), {"chan": (n + m) % chans})
     for j in range(width):
         for m in range(chans):
             arrive(g_place((sib + bands - 2 * j) % bands, (n + chans - m) % chans), ("f", j, m))
@@ -286,16 +291,14 @@
         for t in range(3):
             share[3 * a + t] = rows[:, t * rows_i:(t + 1) * rows_i] * scale
 
-    side = z // 2
-
-    def spot(t, part, bb):
-        return o_ref.at[t, part, :, ds(bb * rows_i, rows_i)]
-
-    def spread(t, part, step):
-        place = spot(t, part, b)
+    def spot(t, bb):
+        return o_ref.at[t, :, :, ds(bb * rows_i, rows_i)]
+
+    def spread(t):
+        place = spot(t, b)
         for j in range(1, width):
-            send(place, place, ("xo", t, step, j), {"band": (b + 2 * j) % bands})
-        send(place, place, ("c", t, step, 0), sib_id)
+            send(place, place, ("xo", t, j), {"band": (b + 2 * j) % bands})
+        send(place, place, ("c", t, 0), sib_id)
 
     def give(t):
         for part in range(2):
@@ -305,41 +308,33 @@
     def take(t):
         arrive(got1.at[t], ("r1", t))
         for part in range(2):
-            share[t, part * half:(part + 1) * half, :] += decode(got1[t, part])
-        encode(coded, (t, 0), share[t, ds((1 - side) * half, half), :])
-        send(coded.at[t, 0], got2.at[t], ("r2", t), middle)
+            encode(coded, (t, part), share[t, part * half:(part + 1) * half, :] + decode(got1[t, part]))
+        send(coded.at[t], got2.at[t], ("r2", t), middle)
 
     def settle(t):
         arrive(got2.at[t], ("r2", t))
-        encode(coded, (t, 1), share[t, ds(side * half, half), :] + decode(got2[t]))
-        place = spot(t, side, b)
-        place[...] = coded[t, 1]
-        send(coded.at[t, 1], place, ("a1", t), middle)
-        send(coded.at[t, 1], place, ("a2", t, 0), near)
-        spread(t, side, 0)
-
-    def share_back(t):
-        place = spot(t, 1 - side, b)
-        arrive(place, ("a1", t))
-        send(place, place, ("a2", t, 1), near)
-        spread(t, 1 - side, 1)
+        for part in range(2):
+            encode(final, (t, part), decode(coded[t, part]) + decode(got2[t, part]))
+        place = spot(t, b)
+        send(final.at[t], place, ("a2", t), near)
+        for j in range(1, width):
+            send(final.at[t], place, ("xo", t, j), {"band": (b + 2 * j) % bands})
+        send(final.at[t], place, ("c", t, 0), sib_id)
+        place[...] = final[t]
 
     def receive(t):
-        for step, part in enumerate((side, 1 - side)):
-            arrive(spot(t, part, b), ("a2", t, step))
-            spread(t, part, step)
+        arrive(spot(t, b), ("a2", t))
+        spread(t)
 
     def cross(t):
-        for step, part in enumerate((side, 1 - side)):
-            for j in range(1, width):
-                place = spot(t, part, (b + bands - 2 * j) % bands)
-                arrive(place, ("xo", t, step, j))
-                send(place, place, ("c", t, step, j), sib_id)
+        for j in range(1, width):
+            place = spot(t, (b + bands - 2 * j) % bands)
+            arrive(place, ("xo", t, j))
+            send(place, place, ("c", t, j), sib_id)
 
     def finish(t):
-        for step, part in enumerate((side, 1 - side)):
-            for j in range(width):
-                arrive(spot(t, part, (sib + bands - 2 * j) % bands), ("c", t, step, j))
+        for j in range(width):
+            arrive(spot(t, (sib + bands - 2 * j) % bands), ("c", t, j))
 
     def bias_sum():
         ones = jnp.ones((8, block), BF16)
@@ -379,25 +374,55 @@
         if not split:
             keep_w.wait()
 
+    def weights_late():
+        for m in range(1, chans):
+            src = (n + chans - m) % chans
+            arrive(late(src, core), ("wl", m))
+            send(late(src, core), late(src, core), ("wls", m), sib_id)
+
+    def weights_there():
+        for m in range(1, chans):
+            arrive(late((n + chans - m) % chans, 1 - core), ("wls", m))
+
     def back_out():
         @pl.loop(0, cells // 128)
         def _(t):
             back_ref[:, ds(t * 128, 128)] = acc_b[ds(t * 128, 128), :].T.astype(BF16)
 
+    def back_rows(row):
+        for lo in (0, cells // 2):
+            yield back_part(other, rows_o, lo, lo + cells // 2, (2 - row,), True)
+
     def matmuls():
         yield bias_sum()
+        if not split:
+            halos()
+            weights()
+            weights_late()
+            weights_there()
+            for lo, hi in ((0, cut), (cut, cells - cut), (cells - cut, cells)):
+                yield conv_part(acc_f, 0, channels // 256, lo, hi, (0, 1, 2), False, True)
+            for lo in (0, cells // 2):
+                yield back_part(0, channels, lo, lo + cells // 2, (0, 1, 2), False)
+            yield back_out()
+            return
+        yield weights()
+        yield conv_part(acc_o, other, stripe, 0, cut, (1,), False, False)
+        yield conv_part(acc_o, other, stripe, cut, cells, (1,), False, False)
+        yield from back_rows(1)
+        yield conv_part(acc_o, other, stripe, cut, cells, (0,), True, False)
         yield halos()
-        first, size, count = (other, rows_o, stripe) if split else (0, channels, channels // 256)
-        if split:
-            yield conv_part(own, stripe, 0, cut, (0,), True, True)
-            yield conv_part(own, stripe, cells - cut, cells, (2,), True, True)
-            yield back_part(own, rows_o, 0, W, (0,), True)
-            yield back_part(own, rows_o, cells - W, cells, (2,), True)
-        yield weights()
-        for lo, hi in ((0, cut), (cut, cells - cut), (cells - cut, cells)):
-            yield conv_part(first, count, lo, hi, (0, 1, 2), False, True)
-        for lo in (0, cells // 2):
-            yield back_part(first, size, lo, lo + cells // 2, (0, 1, 2), split)
+        yield conv_part(acc_f, own, stripe, 0, cut, (0,), True, True)
+        yield conv_part(acc_f, own, stripe, cells - cut, cells, (2,), True, True)
+        yield back_part(own, rows_o, 0, W, (0,), True)
+        yield back_part(own, rows_o, cells - W, cells, (2,), True)
+        yield conv_part(acc_o, other, stripe, 0, cut, (0,), True, False)
+        yield from back_rows(0)
+        weights_late()
+        yield weights_there()
+        yield conv_part(acc_o, other, stripe, 0, cut, (2,), True, True)
+        yield conv_part(acc_o, other, stripe, cut, cells, (2,), True, True)
+        yield from back_rows(2)
         yield back_out()
 
     gathered = list(started)
@@ -411,13 +436,13 @@
                 for t in range(3 * a, 3 * a + 3):
                     give(t)
         if role:
-            for t in range(13):
-                for step, lag in ((take, 0), (settle, 1), (share_back, 2), (cross, 4)):
+            for t in range(12):
+                for step, lag in ((take, 0), (settle, 1), (cross, 3)):
                     if 0 <= t - lag < 9:
                         step(t - lag)
                 next(work, None)
         else:
-            for _ in range(3):
+            for _ in range(6):
                 next(work, None)
             for t in range(11):
                 for step, lag in ((receive, 0), (cross, 2)):
@@ -490,7 +515,7 @@
     wt = jnp.transpose(weight, (1, 2, 0, 3)).reshape(9, rows_o, channels)
     half = rows_o // 2
     width = bands // 2
-    copies = (chans - 1) * (1 + clips - 1 + clips) + 2 * width * chans + group + bands * chans + 4 + clips + 9 * (5 + 4 * width) + 8
+    copies = (chans - 1) * (1 + clips - 1 + clips) + 2 * width * chans + group + bands * chans + 4 + clips + 9 * (5 + 4 * width) + 8 + 4 * chans
     limit = (24 << 20) + (total + 2 * W) * 4 * rows_i * 2 + rows_o * total * 2 + rows_o * channels * 72
     shape = jax.ShapeDtypeStruct
     result = pltpu.VMEM if limit < (50 << 20) else shape
@@ -512,11 +537,13 @@
             pltpu.VMEM((cells + 2 * W, 3 * channels), BF16),
             pltpu.VMEM((9, channels, channels), BF16),
             pltpu.VMEM((rows_o, cells), F32),
+            pltpu.VMEM((rows_o, cells), F32),
             pltpu.VMEM((cells, channels), F32),
             pltpu.VMEM((9, rows_o, rows_i), F32),
             pltpu.VMEM((9, 2, half + 16, rows_i), BF16),
             pltpu.VMEM((9, 2, half + 16, rows_i), BF16),
-            pltpu.VMEM((9, half + 16, rows_i), BF16),
+            pltpu.VMEM((9, 2, half + 16, rows_i), BF16),
+            pltpu.VMEM((9, 2, half + 16, rows_i), BF16),
             pltpu.VMEM((8, rows_o), F32),
             pltpu.VMEM((clips, 8, rows_o), F32),
             pltpu.VMEM((2, W, channels), BF16),

time: 83.9 us -> 76.7 us (0.914)
  Pallas kernels: 82.9 us -> 75.7 us
    pallas_call x1, Pallas kernels: 79.9 us -> 72.7 us  [local(): pl.pallas_call(functools.partial(kernel, (clips, bands, chans, rows_o, ro...]
where the time goes in v3:
time: 76.7 us; the launch traced here: 76.5 us
  Pallas kernels  75.7 us (99%)
  between operations  0.82 us (1%)
    pallas_call x1, Pallas kernels, local(): pl.pallas_call(functools.partial(kernel, (clips, bands, chans, rows_o, ro...  72.7 us
    pallas_call x1, Pallas kernels, local(): pl.pallas_call(emit, out_shape=(shape((9, rows_o, channels), F32),) + tup...  3.02 us

profile of v3, /device:TPU:0, one launch (start us, length us, event | category | flops | bytes accessed | tf_op | source)
XLA Modules:
  0.0 76.5 jit_solution(12250865829306428500)
XLA Ops:
  0.6 72.7 %shard_map.75 = (bf16[9,2,144,512]{3,2,1,0:T(8,128)(2,1)S(1)}, f32[1,256]{1,0:T(1,128)S(1)}, bf16[512,640]{1,0:T(8,128)(2,1)S(1)}, bf16[512,640]{1,0:T(8,128)(2,1)S(1)}) custom-call(bf16[512,640]{1,0:T(8,128)(2,1)} %bitcast.13, bf16[512,640]{1,0:T(8,128)(2,1)} %bitcast.14, bf16[9,256,512]{2,1,0:T(8,128)(2,1)} %bitcast.12, f32[1,512]{1,0:T(1,128)} %bitcast.15), custom_call_target="tpu_custom_call" | custom-call | tf_op jit(solution)/shard_map/pallas_call | solution.py:522
  73.3 3.0 %shard_map.76 = (f32[9,256,512]{2,1,0:T(8,128)}, f32[1,256]{1,0:T(1,128)}, bf16[512,640]{1,0:T(8,128)(2,1)}, bf16[512,640]{1,0:T(8,128)(2,1)}) custom-call(bf16[9,2,144,512]{3,2,1,0:T(8,128)(2,1)S(1)} %get-tuple-element.12.refs_0_, f32[1,256]{1,0:T(1,128)S(1)} %get-tuple-element.13.refs_1_, bf16[512,640]{1,0:T(8,128)(2,1)S(1)} %get-tuple-element.14.refs_2_, ...), custom_call_target="tpu_custom_call" | custom-call | tf_op jit(solution)/shard_map/pallas_call | solution.py:562
